TPU v7x, 32 devices: a whole 2x2x4 slice. The times are simulated.
32 devices in a mesh: dp: 8 (over z, core), tensor: 4 (over y, x).
Axes of the slice: x: 2, y: 2, z: 4, core: 2. Of those that a mesh axis runs over, the one named last changes fastest.
Arguments:
- block_input: bfloat16 [8192, 2048], P('dp'), may hold values from -6 to 6
- block_owner: int32 [64], P('dp'), may hold values from 0 to 63, as said below
- token_mask: int32 [8192], P('dp'), may hold values from 0 to 1, as said below
- attention_gain: float32 [2048], replicated, may hold values from 0.5 to 1.5
- query_weight: bfloat16 [2048, 2048], P(None, 'tensor')
- key_weight: bfloat16 [2048, 2048], P(None, 'tensor')
- value_weight: bfloat16 [2048, 2048], P(None, 'tensor'), may hold values from -0.125 to 0.125
- output_weight: bfloat16 [2048, 2048], P('tensor'), may hold values from -0.5 to 0.5
- feedforward_gain: float32 [2048], replicated, may hold values from 0.5 to 1.5
- gate_weight: bfloat16 [2048, 8192], P(None, 'tensor'), may hold values from -0.125 to 0.125
- up_weight: bfloat16 [2048, 8192], P(None, 'tensor'), may hold values from -0.125 to 0.125
- down_weight: bfloat16 [8192, 2048], P('tensor'), may hold values from -0.0625 to 0.0625
- cotangent: bfloat16 [8192, 2048], P('dp'), may hold values from -6 to 6
Outputs:
- block_output: bfloat16 [8192, 2048], P('dp')
- input_gradient: float32 [8192, 2048], P('dp')
- attention_gain_gradient: float32 [2048], P('dp')
- query_gradient: float32 [2048, 2048], P('dp', 'tensor')
- key_gradient: float32 [2048, 2048], P('dp', 'tensor')
- value_gradient: float32 [2048, 2048], P('dp', 'tensor')
- output_gradient: float32 [2048, 2048], P('tensor', 'dp')
- feedforward_gain_gradient: float32 [2048], P('dp')
- gate_gradient: float32 [2048, 8192], P('dp', 'tensor')
- up_gradient: float32 [2048, 8192], P('dp', 'tensor')
- down_gradient: float32 [8192, 2048], P('tensor', 'dp')
Inputs may be any that keep to these rules, and one draw needn't show every extreme that they name: `block_owner`: each sequence takes one to 4 consecutive blocks of a single index of dp; a block's entry is the index of its sequence's first block in the whole array. The first 4 blocks of every index of dp form one sequence. `token_mask`: in each sequence the real tokens come first and there is at least one unless the sequence is a single block of padding; the first sequence of every index of dp is all real (512 tokens). Blocks after the last real token of an index of dp are padding, each its own sequence.
All inputs are finite; a program needn't handle non-finite values.
Results may differ from a plain program's by a relative error of at most 0.014.
Values sent between devices are 32-bit elements; how exact they have to be, the bound alone decides.
No kernel may reach another device: no remote copies, remote signals or barrier semaphores. Data moves between devices by JAX's collectives and lax.ppermute only.
A program may use at most 384 MiB of HBM per device.

v0:
```python
import jax
import jax.numpy as jnp
from jax import lax
from jax.sharding import PartitionSpec as P

HD = 64
BLK = 128
GROUP = 512
WINDOW = 896
NORM_EPS = 1e-05
ROPE_BASE = 130000.0
MASKED = -1e30


def rms_forward(values, norm_gain):
    inverse = lax.rsqrt(jnp.mean(values * values, axis=-1, keepdims=True) + NORM_EPS)
    return (values * inverse * norm_gain, inverse)


def rms_backward(values, inverse, norm_gain, upstream):
    unit_rows = values * inverse
    gain_part = jnp.sum(upstream * unit_rows, axis=0)
    scaled = upstream * norm_gain
    back = inverse * (scaled - unit_rows * jnp.mean(scaled * unit_rows, axis=-1, keepdims=True))
    return (back, gain_part)


def rope_tables(positions, width):
    half_width = width // 2
    frequency = ROPE_BASE ** (-(jnp.arange(half_width, dtype=jnp.float32) * 2.0 / width))
    angles = positions.astype(jnp.float32)[:, None] * frequency[None, :]
    return (jnp.cos(angles)[:, None, :], jnp.sin(angles)[:, None, :])


def rotate(values, cosine, sine):
    half_width = values.shape[-1] // 2
    first_half = values[..., :half_width]
    second_half = values[..., half_width:]
    return jnp.concatenate(
        [first_half * cosine - second_half * sine, second_half * cosine + first_half * sine],
        axis=-1,
    )


def allowed_keys(query_owner, query_pos, key_owner, key_pos, key_valid):
    same = query_owner[:, None] == key_owner[None, :]
    causal = key_pos[None, :] <= query_pos[:, None]
    usable = (key_valid[None, :] > 0) | (key_pos[None, :] == 0)
    return same & causal & usable


def masked_scores(query_block, key_block, allowed, scale):
    scores = (
        jnp.einsum("qhd,khd->hqk", query_block, key_block, preferred_element_type=jnp.float32)
        * scale
    )
    return jnp.where(allowed[None], scores, MASKED)


def on_device(
    block_input,
    block_owner,
    token_mask,
    attention_gain,
    query_weight,
    key_weight,
    value_weight,
    output_weight,
    feedforward_gain,
    gate_weight,
    up_weight,
    down_weight,
    cotangent,
):
    row_count = block_input.shape[0]
    head_count = query_weight.shape[1] // HD
    scale = HD ** (-0.5)
    front = WINDOW - GROUP
    group_count = row_count // GROUP
    first_block = lax.axis_index("dp") * (row_count // BLK)
    owners = jnp.repeat(block_owner, BLK, total_repeat_length=row_count)
    row_index = jnp.arange(row_count, dtype=jnp.int32)
    positions = (row_index // BLK + first_block - owners) * BLK + row_index % BLK
    cosine, sine = rope_tables(positions, HD)
    key_owner = jnp.concatenate([jnp.full((front,), -1, jnp.int32), owners])
    key_pos = jnp.concatenate([jnp.zeros((front,), jnp.int32), positions])
    key_valid = jnp.concatenate([jnp.zeros((front,), jnp.int32), token_mask])
    group_masks = []
    for group in range(group_count):
        start = group * GROUP
        group_masks.append(
            allowed_keys(
                owners[start : start + GROUP],
                positions[start : start + GROUP],
                key_owner[start : start + WINDOW],
                key_pos[start : start + WINDOW],
                key_valid[start : start + WINDOW],
            )
        )
    inputs_f = block_input.astype(jnp.float32)
    normed_one, inverse_one = rms_forward(inputs_f, attention_gain)
    act_one = normed_one.astype(jnp.bfloat16)

    def project(weight):
        return jnp.dot(act_one, weight, preferred_element_type=jnp.float32).reshape(
            row_count, head_count, HD
        )

    queries = rotate(project(query_weight), cosine, sine).astype(jnp.bfloat16)
    keys_rot = rotate(project(key_weight), cosine, sine).astype(jnp.bfloat16)
    values_b = project(value_weight).astype(jnp.bfloat16)
    pad_block = jnp.zeros((front, head_count, HD), jnp.bfloat16)
    key_pad = jnp.concatenate([pad_block, keys_rot], axis=0)
    value_pad = jnp.concatenate([pad_block, values_b], axis=0)
    attn_list = []
    logsum_list = []
    for group in range(group_count):
        start = group * GROUP
        scores = masked_scores(
            queries[start : start + GROUP],
            key_pad[start : start + WINDOW],
            group_masks[group],
            scale,
        )
        peak = jnp.max(scores, axis=-1, keepdims=True)
        logsum = peak + jnp.log(jnp.sum(jnp.exp(scores - peak), axis=-1, keepdims=True))
        probs = jnp.exp(scores - logsum).astype(jnp.bfloat16)
        result = jnp.einsum(
            "hqk,khd->qhd",
            probs,
            value_pad[start : start + WINDOW],
            preferred_element_type=jnp.float32,
        )
        attn_list.append(result.astype(jnp.bfloat16))
        logsum_list.append(logsum)
    attn_heads = jnp.concatenate(attn_list, axis=0)
    attn_flat = attn_heads.reshape(row_count, head_count * HD)
    attn_part = jnp.dot(attn_flat, output_weight, preferred_element_type=jnp.float32)
    attn_total = lax.psum(attn_part, "tensor")
    hidden_sum = inputs_f + attn_total
    normed_two, inverse_two = rms_forward(hidden_sum, feedforward_gain)
    act_two = normed_two.astype(jnp.bfloat16)
    gate_pre = jnp.dot(act_two, gate_weight, preferred_element_type=jnp.float32)
    up_pre = jnp.dot(act_two, up_weight, preferred_element_type=jnp.float32)
    sigmoid_gate = jax.nn.sigmoid(gate_pre)
    inner = (gate_pre * sigmoid_gate * up_pre).astype(jnp.bfloat16)
    mlp_part = jnp.dot(inner, down_weight, preferred_element_type=jnp.float32)
    mlp_total = lax.psum(mlp_part, "tensor")
    block_output = (hidden_sum + mlp_total).astype(jnp.bfloat16)
    grad_rows = jnp.where(token_mask[:, None] > 0, cotangent, jnp.zeros_like(cotangent))
    down_grad = jnp.dot(inner.T, grad_rows, preferred_element_type=jnp.float32)
    inner_grad = jnp.dot(grad_rows, down_weight.T, preferred_element_type=jnp.float32)
    gate_back = (
        inner_grad * up_pre * sigmoid_gate * (1.0 + gate_pre * (1.0 - sigmoid_gate))
    ).astype(jnp.bfloat16)
    up_back = (inner_grad * gate_pre * sigmoid_gate).astype(jnp.bfloat16)
    gate_grad = jnp.dot(act_two.T, gate_back, preferred_element_type=jnp.float32)
    up_grad = jnp.dot(act_two.T, up_back, preferred_element_type=jnp.float32)
    act_two_part = jnp.dot(gate_back, gate_weight.T, preferred_element_type=jnp.float32) + jnp.dot(
        up_back, up_weight.T, preferred_element_type=jnp.float32
    )
    act_two_grad = lax.psum(act_two_part, "tensor")
    hidden_norm_back, second_gain_grad = rms_backward(
        hidden_sum, inverse_two, feedforward_gain, act_two_grad
    )
    hidden_grad = grad_rows.astype(jnp.float32) + hidden_norm_back
    mlp_summed = (
        lax.psum_scatter(gate_grad, "dp", scatter_dimension=0, tiled=True),
        lax.psum_scatter(up_grad, "dp", scatter_dimension=0, tiled=True),
        lax.psum_scatter(down_grad, "dp", scatter_dimension=1, tiled=True),
        lax.psum_scatter(second_gain_grad, "dp", scatter_dimension=0, tiled=True),
    )
    hidden_back = hidden_grad.astype(jnp.bfloat16)
    out_grad = jnp.dot(attn_flat.T, hidden_back, preferred_element_type=jnp.float32)
    attention_grad = (
        jnp.dot(hidden_back, output_weight.T, preferred_element_type=jnp.float32)
        .astype(jnp.bfloat16)
        .reshape(row_count, head_count, HD)
    )
    key_acc = jnp.zeros((front + row_count, head_count, HD), jnp.float32)
    value_acc = jnp.zeros((front + row_count, head_count, HD), jnp.float32)
    query_parts = []
    for group in range(group_count):
        start = group * GROUP
        query_block = queries[start : start + GROUP]
        key_block = key_pad[start : start + WINDOW]
        value_block = value_pad[start : start + WINDOW]
        grad_block = attention_grad[start : start + GROUP]
        scores = masked_scores(query_block, key_block, group_masks[group], scale)
        probs_f = jnp.exp(scores - logsum_list[group])
        probs_b = probs_f.astype(jnp.bfloat16)
        value_acc = value_acc.at[start : start + WINDOW].add(
            jnp.einsum("hqk,qhd->khd", probs_b, grad_block, preferred_element_type=jnp.float32)
        )
        prob_grad = jnp.einsum(
            "qhd,khd->hqk", grad_block, value_block, preferred_element_type=jnp.float32
        )
        delta = jnp.sum(
            grad_block.astype(jnp.float32) * attn_heads[start : start + GROUP].astype(jnp.float32),
            axis=-1,
        ).T[:, :, None]
        score_grad = (probs_f * (prob_grad - delta) * scale).astype(jnp.bfloat16)
        query_parts.append(
            jnp.einsum("hqk,khd->qhd", score_grad, key_block, preferred_element_type=jnp.float32)
        )
        key_acc = key_acc.at[start : start + WINDOW].add(
            jnp.einsum("hqk,qhd->khd", score_grad, query_block, preferred_element_type=jnp.float32)
        )
    query_back = (
        rotate(jnp.concatenate(query_parts, axis=0), cosine, -sine)
        .astype(jnp.bfloat16)
        .reshape(row_count, head_count * HD)
    )
    key_back = (
        rotate(key_acc[front:], cosine, -sine)
        .astype(jnp.bfloat16)
        .reshape(row_count, head_count * HD)
    )
    value_back = value_acc[front:].astype(jnp.bfloat16).reshape(row_count, head_count * HD)
    query_grad = jnp.dot(act_one.T, query_back, preferred_element_type=jnp.float32)
    key_grad = jnp.dot(act_one.T, key_back, preferred_element_type=jnp.float32)
    value_grad = jnp.dot(act_one.T, value_back, preferred_element_type=jnp.float32)
    act_one_part = (
        jnp.dot(query_back, query_weight.T, preferred_element_type=jnp.float32)
        + jnp.dot(key_back, key_weight.T, preferred_element_type=jnp.float32)
        + jnp.dot(value_back, value_weight.T, preferred_element_type=jnp.float32)
    )
    act_one_grad = lax.psum(act_one_part, "tensor")
    input_norm_back, first_gain_grad = rms_backward(
        inputs_f, inverse_one, attention_gain, act_one_grad
    )
    input_gradient = hidden_grad + input_norm_back
    first_summed = (
        lax.psum_scatter(first_gain_grad, "dp", scatter_dimension=0, tiled=True),
        lax.psum_scatter(query_grad, "dp", scatter_dimension=0, tiled=True),
        lax.psum_scatter(key_grad, "dp", scatter_dimension=0, tiled=True),
        lax.psum_scatter(value_grad, "dp", scatter_dimension=0, tiled=True),
        lax.psum_scatter(out_grad, "dp", scatter_dimension=1, tiled=True),
    )
    gate_sum, up_sum, down_sum, second_gain_sum = mlp_summed
    first_gain_sum, query_sum, key_sum, value_sum, out_sum = first_summed
    return (
        block_output,
        input_gradient,
        first_gain_sum,
        query_sum,
        key_sum,
        value_sum,
        out_sum,
        second_gain_sum,
        gate_sum,
        up_sum,
        down_sum,
    )


def solution(mesh):
    return jax.shard_map(
        on_device,
        mesh=mesh,
        in_specs=(
            P("dp", None),
            P("dp"),
            P("dp"),
            P(),
            P(None, "tensor"),
            P(None, "tensor"),
            P(None, "tensor"),
            P("tensor", None),
            P(),
            P(None, "tensor"),
            P(None, "tensor"),
            P("tensor", None),
            P("dp", None),
        ),
        out_specs=(
            P("dp", None),
            P("dp", None),
            P("dp"),
            P("dp", "tensor"),
            P("dp", "tensor"),
            P("dp", "tensor"),
            P("tensor", "dp"),
            P("dp"),
            P("dp", "tensor"),
            P("dp", "tensor"),
            P("tensor", "dp"),
        ),
        check_vma=False,
    )
```

profile of v0, /device:TPU:0, one launch (start us, length us, event | category | flops | bytes accessed | tf_op | source)
XLA Modules:
  0.0 1614.1 jit_solution(13321575594222905438)
XLA Ops:
  71.6 174.8 %all-reduce.15.cloned.1.call-done = f32[1024,2048]{1,0:T(8,128)} async-done(((f32[1024,2048]{1,0:T(8,128)}), f32[1024,2048]{1,0:T(8,128)}) %all-reduce.15.cloned.1.call-update) | async-done | bytes 8388624 | tf_op jit(solution)/shard_map/psum | solution.py:139
  253.0 16.5 %fusion.82 = f32[1024,2048]{1,0:T(8,128)} fusion(bf16[1024,2048]{1,0:T(8,128)(2,1)S(1)} %multiply_convert_fusion.5, bf16[2048,2048]{1,0:T(8,128)(2,1)} %param.32), kind=kOutput, calls=%fused_computation.154 | convolution fusion | flops 8589934592 | bytes 20971520 | tf_op jit(solution)/shard_map/dot_general | solution.py:143
  269.5 13.3 fusion.83
  282.9 21.9 %multiply_convert_fusion.2 = (bf16[1024,2048]{1,0:T(8,128)(2,1)}, bf16[1024,2048]{1,0:T(8,128)(2,1)}, bf16[1024,2048]{1,0:T(8,128)(2,1)}) fusion(f32[1024,2048]{1,0:T(8,128)} %fusion.82, f32[1024,2048]{1,0:T(8,128)} %fusion.83, bf16[2048,2048]{1,0:T(8,128)(2,1)} %param.34, bf16[1024,2048]{1,0:T(8,128)(2,1)} %param.35, ...), kind=kOutput, calls=%fused_computation.30 | convolution fusion | flops 8625586176 | bytes 41944064 | tf_op jit(solution)/shard_map/dot_general | solution.py:152
  304.8 13.1 fusion.85
  317.9 13.6 convolution_add_fusion
  331.6 14.7 fusion.84
  346.3 158.2 %all-reduce.17.cloned.1.call-done = f32[1024,2048]{1,0:T(8,128)} async-done(((f32[1024,2048]{1,0:T(8,128)}), f32[1024,2048]{1,0:T(8,128)}) %all-reduce.17.cloned.1.call-update) | async-done | bytes 8388624 | tf_op jit(solution)/shard_map/psum | solution.py:162
  512.1 9.5 multiply_add_fusion
  555.4 9.1 multiply_convert_fusion
  590.1 7.8 fusion.15
  612.6 15.6 fusion.88
  628.3 15.5 fusion.89
  644.2 15.6 fusion.62
  661.7 228.7 %all-reduce.19.cloned.1.call-done = (f32[1024,2048]{1,0:T(8,128)}, f32[1024,2048]{1,0:T(8,128)}) async-done(((f32[1024,2048]{1,0:T(8,128)}, f32[1024,2048]{1,0:T(8,128)}), (f32[1024,2048]{1,0:T(8,128)}, f32[1024,2048]{1,0:T(8,128)})) %all-reduce.19.cloned.1.call-update) | async-done | bytes 16777232 | tf_op jit(solution)/shard_map/psum | solution.py:148
  896.2 29.6 %all-reduce.9 = (f32[2048]{0:T(1024)S(1)}, f32[2048]{0:T(1024)S(1)}) all-reduce(f32[2048]{0:T(1024)S(1)} %get-tuple-element.73, f32[2048]{0:T(1024)S(1)} %copy-done.47), channel_id=2, replica_groups=mesh['dp'=8,'tensor'=4] {'dp'}, use_global_device_ids=true, to_apply=%region_15.16.clone | all-reduce | flops 4096 | bytes 32768
  927.1 9.6 add_convert_fusion
  936.7 9.8 fusion.12
  946.6 49.2 %reduce-scatter.14.cloned.1.call-done = f32[512,256]{1,0:T(8,128)} async-done(((f32[512,2048]{1,0:T(8,128)}), f32[512,256]{1,0:T(8,128)}) %reduce-scatter.14.cloned.1.call-update) | async-done | bytes 524304 | tf_op jit(solution)/shard_map/reduce_scatter | solution.py:238
  995.8 51.1 %reduce-scatter.10.cloned.1.call-done = f32[256,512]{1,0:T(8,128)} async-done(((f32[2048,512]{1,0:T(8,128)}), f32[256,512]{1,0:T(8,128)}) %reduce-scatter.10.cloned.1.call-update) | async-done | bytes 524304 | tf_op jit(solution)/shard_map/reduce_scatter | solution.py:236
  1046.9 51.3 %reduce-scatter.8.cloned.1.call-done = f32[256,512]{1,0:T(8,128)} async-done(((f32[2048,512]{1,0:T(8,128)}), f32[256,512]{1,0:T(8,128)}) %reduce-scatter.8.cloned.1.call-update) | async-done | bytes 524304 | tf_op jit(solution)/shard_map/reduce_scatter | solution.py:235
  1098.2 169.6 %reduce-scatter.16.cloned.1.call-done = f32[256,2048]{1,0:T(8,128)} async-done(((f32[2048,2048]{1,0:T(8,128)}), f32[256,2048]{1,0:T(8,128)}) %reduce-scatter.16.cloned.1.call-update) | async-done | bytes 2097168 | tf_op jit(solution)/shard_map/reduce_scatter | solution.py:168
  1267.8 169.6 %reduce-scatter.18.cloned.1.call-done = f32[256,2048]{1,0:T(8,128)} async-done(((f32[2048,2048]{1,0:T(8,128)}), f32[256,2048]{1,0:T(8,128)}) %reduce-scatter.18.cloned.1.call-update) | async-done | bytes 2097168 | tf_op jit(solution)/shard_map/reduce_scatter | solution.py:169
  1437.4 169.4 %reduce-scatter.20.cloned.1.call-done = f32[2048,256]{1,0:T(8,128)} async-done(((f32[2048,2048]{1,0:T(8,128)}), f32[2048,256]{1,0:T(8,128)}) %reduce-scatter.20.cloned.1.call-update) | async-done | bytes 2097168 | tf_op jit(solution)/shard_map/reduce_scatter | solution.py:170
  (212 shorter events, 160.4 us)
Async XLA Ops:
  7.2 58.5 %copy-start = (bf16[512,2048]{1,0:T(8,128)(2,1)S(1)}, bf16[512,2048]{1,0:T(8,128)(2,1)}, u32[]{:S(2)}) copy-start(bf16[512,2048]{1,0:T(8,128)(2,1)} %param.30) | copy-start | bytes 6291460
  7.2 239.3 %all-reduce.15.cloned.1.call-start = ((), (), s32[]{:S(2)}) async-start(), calls=%async_computation.7 | async-start | bytes 16777216 | tf_op jit(solution)/shard_map/psum | solution.py:139
  17.2 17.6 %copy-start.44 = (f32[1024]{0:T(1024)}, f32[1024]{0:T(1024)S(1)}, u32[]{:S(2)}) copy-start(f32[1024]{0:T(1024)S(1)} %add_rsqrt_fusion.1) | copy-start | bytes 12292
  28.0 24.2 %copy-start.19 = (pred[512,896]{1,0:T(8,128)(4,1)}, pred[512,896]{1,0:T(8,128)(4,1)S(1)}, u32[]{:S(2)}) copy-start(pred[512,896]{1,0:T(8,128)(4,1)S(1)} %and_and_fusion.1) | copy-start | bytes 1376260
  30.8 21.4 %copy-start.5 = (f32[8,512,896]{2,1,0:T(8,128)}, f32[8,512,896]{2,1,0:T(8,128)S(1)}, u32[]{:S(2)}) copy-start(f32[8,512,896]{2,1,0:T(8,128)S(1)} %get-tuple-element.127) | copy-start | bytes 44040196
  34.8 17.4 %copy-start.52 = (f32[8,512]{1,0:T(8,128)}, f32[8,512]{1,0:T(8,128)S(1)}, u32[]{:S(2)}) copy-start(f32[8,512]{1,0:T(8,128)S(1)} %log_add_fusion.1) | copy-start | bytes 49156
  38.0 18.4 %copy-start.27 = (pred[512,896]{1,0:T(8,128)(4,1)}, pred[512,896]{1,0:T(8,128)(4,1)S(1)}, u32[]{:S(2)}) copy-start(pred[512,896]{1,0:T(8,128)(4,1)S(1)} %and_and_fusion) | copy-start | bytes 1376260
  71.5 432.9 %all-reduce.17.cloned.1.call-start = ((), (), s32[]{:S(2)}) async-start(), calls=%async_computation.8 | async-start | bytes 16777216 | tf_op jit(solution)/shard_map/psum | solution.py:162
  71.6 180.6 %copy-start.43 = (f32[2048]{0:T(1024)S(1)}, f32[2048]{0:T(1024)}, u32[]{:S(2)}) copy-start(f32[2048]{0:T(1024)} %param.31) | copy-start | bytes 24580
  252.2 17.4 %copy-start.2 = (f32[1024,2048]{1,0:T(8,128)}, f32[1024,2048]{1,0:T(8,128)S(1)}, u32[]{:S(2)}) copy-start(f32[1024,2048]{1,0:T(8,128)S(1)} %get-tuple-element.82) | copy-start | bytes 25165828
  331.5 558.8 %all-reduce.19.cloned.1.call-start = ((), (), s32[]{:S(2)}) async-start(), calls=%async_computation.16 | async-start | bytes 33554432 | tf_op jit(solution)/shard_map/psum | solution.py:148
  512.1 16.7 %slice-start = ((s8[14680064]{0:T(1024)(128)(4,1)}), s8[4194304]{0:T(1024)(128)(4,1)S(1)}, s32[]{:S(2)}) async-start(s8[14680064]{0:T(1024)(128)(4,1)} %bitcast.98), calls=%async_computation.17 | async-start | bytes 8388608
  512.1 16.7 %slice-start.1 = ((s8[14680064]{0:T(1024)(128)(4,1)}), s8[4194304]{0:T(1024)(128)(4,1)S(1)}, s32[]{:S(2)}) async-start(s8[14680064]{0:T(1024)(128)(4,1)} %bitcast.98), calls=%async_computation.18 | async-start | bytes 8388608
  512.1 16.7 %slice-start.2 = ((s8[14680064]{0:T(1024)(128)(4,1)}), s8[4194304]{0:T(1024)(128)(4,1)S(1)}, s32[]{:S(2)}) async-start(s8[14680064]{0:T(1024)(128)(4,1)} %bitcast.98), calls=%async_computation.19 | async-start | bytes 8388608
  528.4 19.3 %copy-start.42 = (bf16[512,512]{0,1:T(8,128)(2,1)}, bf16[512,512]{0,1:T(8,128)(2,1)S(1)}, u32[]{:S(2)}) copy-start(bf16[512,512]{0,1:T(8,128)(2,1)S(1)} %get-tuple-element.98) | copy-start | bytes 1572868
  582.2 364.4 %reduce-scatter.12.cloned.1.call-start = ((), (), s32[]{:S(2)}) async-start(), calls=%async_computation.11 | async-start | bytes 4718592 | tf_op jit(solution)/shard_map/reduce_scatter | solution.py:237
  590.1 405.7 %reduce-scatter.14.cloned.1.call-start = ((), (), s32[]{:S(2)}) async-start(), calls=%async_computation.12 | async-start | bytes 4718592 | tf_op jit(solution)/shard_map/reduce_scatter | solution.py:238
  597.9 449.0 %reduce-scatter.10.cloned.1.call-start = ((), (), s32[]{:S(2)}) async-start(), calls=%async_computation.10 | async-start | bytes 4718592 | tf_op jit(solution)/shard_map/reduce_scatter | solution.py:236
  605.0 493.2 %reduce-scatter.8.cloned.1.call-start = ((), (), s32[]{:S(2)}) async-start(), calls=%async_computation.9 | async-start | bytes 4718592 | tf_op jit(solution)/shard_map/reduce_scatter | solution.py:235
  612.4 655.4 %reduce-scatter.16.cloned.1.call-start = ((), (), s32[]{:S(2)}) async-start(), calls=%async_computation.13 | async-start | bytes 18874368 | tf_op jit(solution)/shard_map/reduce_scatter | solution.py:168
  628.3 809.1 %reduce-scatter.18.cloned.1.call-start = ((), (), s32[]{:S(2)}) async-start(), calls=%async_computation.14 | async-start | bytes 18874368 | tf_op jit(solution)/shard_map/reduce_scatter | solution.py:169
  643.9 963.0 %reduce-scatter.20.cloned.1.call-start = ((), (), s32[]{:S(2)}) async-start(), calls=%async_computation.15 | async-start | bytes 18874368 | tf_op jit(solution)/shard_map/reduce_scatter | solution.py:170
  659.8 236.4 %copy-start.47 = (f32[2048]{0:T(1024)S(1)}, f32[2048]{0:T(1024)}, u32[]{:S(2)}) copy-start(f32[2048]{0:T(1024)} %get-tuple-element.71) | copy-start | bytes 24580
  927.1 679.7 %copy-start.1 = (bf16[512,2048]{1,0:T(8,128)(2,1)S(1)}, bf16[512,2048]{1,0:T(8,128)(2,1)}, u32[]{:S(2)}) copy-start(bf16[512,2048]{1,0:T(8,128)(2,1)} %param.30) | copy-start | bytes 6291460
  (49 other events, 282.6 us)
Sparse Core Ops, SparseCore 0:
  71.7 174.7 all-reduce.14
  331.7 172.7 all-reduce.16
  582.3 308.0 all-reduce.18
  893.1 51.4 reduce-scatter.11
  947.3 48.4 reduce-scatter.13
  998.5 48.3 reduce-scatter.9
  1049.8 48.3 reduce-scatter.7
  1101.2 166.6 reduce-scatter.15
  1270.8 166.6 reduce-scatter.17
  1440.2 166.6 reduce-scatter.19
where the time goes:
time: 1620 us; the launch traced here: 1610 us
  waiting for transfers between devices  1220 us (75%)
  matrix products  263 us (16%)
  other arithmetic  72.8 us (4%)
  blocking collectives  29.6 us (2%)
  between operations  16.4 us (1%)
    psum x1, waiting for transfers between devices, on_device(): mlp_total = lax.psum(mlp_part, 'tensor')  229 us
    psum x1, waiting for transfers between devices, on_device(): attn_total = lax.psum(attn_part, 'tensor')  175 us
    reduce_scatter x1, waiting for transfers between devices, on_device(): lax.psum_scatter(up_grad, 'dp', scatter_dimension=0, tiled=True)  170 us
    reduce_scatter x1, waiting for transfers between devices, on_device(): lax.psum_scatter(gate_grad, 'dp', scatter_dimension=0, tiled=True)  170 us
    reduce_scatter x1, waiting for transfers between devices, on_device(): lax.psum_scatter(down_grad, 'dp', scatter_dimension=1, tiled=True)  169 us
    psum x1, waiting for transfers between devices, on_device(): act_two_grad = lax.psum(act_two_part, 'tensor')  158 us
    reduce_scatter x1, waiting for transfers between devices, on_device(): lax.psum_scatter(query_grad, 'dp', scatter_dimension=0, tiled=True)  51.3 us
    reduce_scatter x1, waiting for transfers between devices, on_device(): lax.psum_scatter(key_grad, 'dp', scatter_dimension=0, tiled=True)  51.1 us
  transfers between devices with their start and end apart: 10, of which 9 were waited for; matrix products, arithmetic and copies ran while one was open for 7% of the time, Pallas kernels for 0%

commit v1 on v0

--- a/solution.py
+++ b/solution.py
@@ -159,7 +159,13 @@
     act_two_part = jnp.dot(gate_back, gate_weight.T, preferred_element_type=jnp.float32) + jnp.dot(
         up_back, up_weight.T, preferred_element_type=jnp.float32
     )
-    act_two_grad = lax.psum(act_two_part, "tensor")
+    count = lax.axis_size("tensor")
+    act_two_grad, far = (act_two_part, 1)
+    while far < count:
+        act_two_grad = act_two_grad + lax.ppermute(
+            act_two_grad, "tensor", [(i, i ^ far) for i in range(count)]
+        )
+        far = 2 * far
     hidden_norm_back, second_gain_grad = rms_backward(
         hidden_sum, inverse_two, feedforward_gain, act_two_grad
     )

time: 1620 us -> 1840 us (1.14)
  waiting for transfers between devices: 1220 us -> 1410 us
    ppermute x0 -> x2, waiting for transfers between devices: none -> 344 us  [on_device(): lax.ppermute(act_two_grad, 'tensor', [(i, i ^ far) for i in range(count)])]
    psum x1 -> x0, waiting for transfers between devices: 158 us -> none  [on_device(): act_two_grad = lax.psum(act_two_part, 'tensor')]
  transfers between devices with their start and end apart: 10 -> 11, of which waited for: 9 -> 10; matrix products, arithmetic and copies ran while one was open for 7% -> 6% of each run, Pallas kernels for 0% -> 0%
where the time goes in v1:
time: 1840 us; the launch traced here: 1830 us
  waiting for transfers between devices  1410 us (77%)
  matrix products  278 us (15%)
  other arithmetic  83 us (5%)
  blocking collectives  29.6 us (2%)
    ppermute x2, waiting for transfers between devices, on_device(): lax.ppermute(act_two_grad, 'tensor', [(i, i ^ far) for i in range(count)])  344 us
    psum x1, waiting for transfers between devices, on_device(): mlp_total = lax.psum(mlp_part, 'tensor')  229 us
    psum x1, waiting for transfers between devices, on_device(): attn_total = lax.psum(attn_part, 'tensor')  175 us
    reduce_scatter x1, waiting for transfers between devices, on_device(): lax.psum_scatter(down_grad, 'dp', scatter_dimension=1, tiled=True)  170 us
    reduce_scatter x1, waiting for transfers between devices, on_device(): lax.psum_scatter(gate_grad, 'dp', scatter_dimension=0, tiled=True)  170 us
    reduce_scatter x1, waiting for transfers between devices, on_device(): lax.psum_scatter(up_grad, 'dp', scatter_dimension=0, tiled=True)  170 us
    reduce_scatter x1, waiting for transfers between devices, on_device(): lax.psum_scatter(query_grad, 'dp', scatter_dimension=0, tiled=True)  51.1 us
    reduce_scatter x1, waiting for transfers between devices, on_device(): lax.psum_scatter(key_grad, 'dp', scatter_dimension=0, tiled=True)  51.1 us
  transfers between devices with their start and end apart: 11, of which 10 were waited for; matrix products, arithmetic and copies ran while one was open for 6% of the time, Pallas kernels for 0%

profile of v1, /device:TPU:0, one launch (start us, length us, event | category | flops | bytes accessed | tf_op | source)
XLA Modules:
  0.0 1829.9 jit_solution(15961373914016344815)
XLA Ops:
  56.6 18.0 fusion.25
  82.3 174.8 %all-reduce.14.cloned.1.call-done = f32[1024,2048]{1,0:T(8,128)} async-done(((f32[1024,2048]{1,0:T(8,128)}), f32[1024,2048]{1,0:T(8,128)}) %all-reduce.14.cloned.1.call-update) | async-done | bytes 8388624 | tf_op jit(solution)/shard_map/psum | solution.py:139
  263.7 16.6 fusion.82
  280.2 13.3 fusion.83
  293.6 21.9 %multiply_convert_fusion.2 = (bf16[1024,2048]{1,0:T(8,128)(2,1)}, bf16[1024,2048]{1,0:T(8,128)(2,1)}, bf16[1024,2048]{1,0:T(8,128)(2,1)}) fusion(f32[1024,2048]{1,0:T(8,128)} %fusion.82, f32[1024,2048]{1,0:T(8,128)} %fusion.83, bf16[2048,2048]{1,0:T(8,128)(2,1)} %param.34, bf16[1024,2048]{1,0:T(8,128)(2,1)} %param.35, ...), kind=kOutput, calls=%fused_computation.30 | convolution fusion | flops 8625586176 | bytes 41944064 | tf_op jit(solution)/shard_map/dot_general | solution.py:152
  315.5 15.3 fusion.85
  330.8 12.8 convolution_add_fusion
  347.0 178.8 %collective-permute-done = f32[1024,2048]{1,0:T(8,128)} collective-permute-done((f32[1024,2048]{1,0:T(8,128)S(1)}, f32[1024,2048]{1,0:T(8,128)}, u32[]{:S(2)}, u32[]{:S(2)}) %collective-permute-start) | collective-permute-done | bytes 8388640 | tf_op jit(solution)/shard_map/ppermute | solution.py:165
  525.8 11.9 add.249
  539.1 14.8 fusion.84
  553.9 165.4 %collective-permute-done.1 = f32[1024,2048]{1,0:T(8,128)} collective-permute-done((f32[1024,2048]{1,0:T(8,128)}, f32[1024,2048]{1,0:T(8,128)}, u32[]{:S(2)}, u32[]{:S(2)}) %collective-permute-start.1) | collective-permute-done | bytes 8388640 | tf_op jit(solution)/shard_map/ppermute | solution.py:165
  828.6 15.6 fusion.88
  844.3 15.5 fusion.89
  860.1 15.6 fusion.62
  877.7 228.6 %all-reduce.16.cloned.1.call-done = (f32[1024,2048]{1,0:T(8,128)}, f32[1024,2048]{1,0:T(8,128)}) async-done(((f32[1024,2048]{1,0:T(8,128)}, f32[1024,2048]{1,0:T(8,128)}), (f32[1024,2048]{1,0:T(8,128)}, f32[1024,2048]{1,0:T(8,128)})) %all-reduce.16.cloned.1.call-update) | async-done | bytes 16777232 | tf_op jit(solution)/shard_map/psum | solution.py:148
  1112.2 29.6 %all-reduce.9 = (f32[2048]{0:T(1024)S(1)}, f32[2048]{0:T(1024)S(1)}) all-reduce(f32[2048]{0:T(1024)S(1)} %get-tuple-element.73, f32[2048]{0:T(1024)S(1)} %copy-done.49), channel_id=2, replica_groups=mesh['dp'=8,'tensor'=4] {'dp'}, use_global_device_ids=true, to_apply=%region_14.15.clone | all-reduce | flops 4096 | bytes 32768
  1143.1 9.6 add_convert_fusion
  1152.7 9.8 fusion.12
  1162.5 49.4 %reduce-scatter.14.cloned.1.call-done = f32[512,256]{1,0:T(8,128)} async-done(((f32[512,2048]{1,0:T(8,128)}), f32[512,256]{1,0:T(8,128)}) %reduce-scatter.14.cloned.1.call-update) | async-done | bytes 524304 | tf_op jit(solution)/shard_map/reduce_scatter | solution.py:244
  1211.9 51.1 %reduce-scatter.10.cloned.1.call-done = f32[256,512]{1,0:T(8,128)} async-done(((f32[2048,512]{1,0:T(8,128)}), f32[256,512]{1,0:T(8,128)}) %reduce-scatter.10.cloned.1.call-update) | async-done | bytes 524304 | tf_op jit(solution)/shard_map/reduce_scatter | solution.py:242
  1263.0 51.1 %reduce-scatter.8.cloned.1.call-done = f32[256,512]{1,0:T(8,128)} async-done(((f32[2048,512]{1,0:T(8,128)}), f32[256,512]{1,0:T(8,128)}) %reduce-scatter.8.cloned.1.call-update) | async-done | bytes 524304 | tf_op jit(solution)/shard_map/reduce_scatter | solution.py:241
  1314.2 169.6 %reduce-scatter.16.cloned.1.call-done = f32[256,2048]{1,0:T(8,128)} async-done(((f32[2048,2048]{1,0:T(8,128)}), f32[256,2048]{1,0:T(8,128)}) %reduce-scatter.16.cloned.1.call-update) | async-done | bytes 2097168 | tf_op jit(solution)/shard_map/reduce_scatter | solution.py:174
  1483.8 169.6 %reduce-scatter.18.cloned.1.call-done = f32[256,2048]{1,0:T(8,128)} async-done(((f32[2048,2048]{1,0:T(8,128)}), f32[256,2048]{1,0:T(8,128)}) %reduce-scatter.18.cloned.1.call-update) | async-done | bytes 2097168 | tf_op jit(solution)/shard_map/reduce_scatter | solution.py:175
  1653.4 169.6 %reduce-scatter.20.cloned.1.call-done = f32[2048,256]{1,0:T(8,128)} async-done(((f32[2048,2048]{1,0:T(8,128)}), f32[2048,256]{1,0:T(8,128)}) %reduce-scatter.20.cloned.1.call-update) | async-done | bytes 2097168 | tf_op jit(solution)/shard_map/reduce_scatter | solution.py:176
  (223 shorter events, 185.2 us)
Async XLA Ops:
  7.2 69.2 %copy-start = (bf16[512,2048]{1,0:T(8,128)(2,1)S(1)}, bf16[512,2048]{1,0:T(8,128)(2,1)}, u32[]{:S(2)}) copy-start(bf16[512,2048]{1,0:T(8,128)(2,1)} %param.30) | copy-start | bytes 6291460
  7.2 249.9 %all-reduce.14.cloned.1.call-start = ((), (), s32[]{:S(2)}) async-start(), calls=%async_computation.7 | async-start | bytes 16777216 | tf_op jit(solution)/shard_map/psum | solution.py:139
  28.0 24.3 %copy-start.21 = (pred[512,896]{1,0:T(8,128)(4,1)}, pred[512,896]{1,0:T(8,128)(4,1)S(1)}, u32[]{:S(2)}) copy-start(pred[512,896]{1,0:T(8,128)(4,1)S(1)} %and_and_fusion.1) | copy-start | bytes 1376260
  30.8 21.5 %copy-start.6 = (f32[8,512,896]{2,1,0:T(8,128)}, f32[8,512,896]{2,1,0:T(8,128)S(1)}, u32[]{:S(2)}) copy-start(f32[8,512,896]{2,1,0:T(8,128)S(1)} %get-tuple-element.127) | copy-start | bytes 44040196
  38.1 18.4 %copy-start.29 = (pred[512,896]{1,0:T(8,128)(4,1)}, pred[512,896]{1,0:T(8,128)(4,1)S(1)}, u32[]{:S(2)}) copy-start(pred[512,896]{1,0:T(8,128)(4,1)S(1)} %and_and_fusion) | copy-start | bytes 1376260
  56.5 18.1 copy-start.25
  82.2 1024.1 %all-reduce.16.cloned.1.call-start = ((), (), s32[]{:S(2)}) async-start(), calls=%async_computation.15 | async-start | bytes 33554432 | tf_op jit(solution)/shard_map/psum | solution.py:148
  82.2 180.6 %copy-start.45 = (f32[2048]{0:T(1024)S(1)}, f32[2048]{0:T(1024)}, u32[]{:S(2)}) copy-start(f32[2048]{0:T(1024)} %param.31) | copy-start | bytes 24580
  343.6 182.2 %collective-permute-start = (f32[1024,2048]{1,0:T(8,128)S(1)}, f32[1024,2048]{1,0:T(8,128)}, u32[]{:S(2)}, u32[]{:S(2)}) collective-permute-start(f32[1024,2048]{1,0:T(8,128)S(1)} %convolution_add_fusion), channel_id=1, source_target_pairs={{0,1},{1,0},{2,3},{3,2},{4,5},{5,4},{6,7},{7,6},{8,9},{9,8},{10,11... | collective-permute-start | bytes 25165832 | tf_op jit(solution)/shard_map/ppermute | solution.py:165
  525.8 193.4 %slice-start = ((s8[8388608]{0:T(1024)(128)(4,1)}), s8[4194304]{0:T(1024)(128)(4,1)S(1)}, s32[]{:S(2)}) async-start(s8[8388608]{0:T(1024)(128)(4,1)} %bitcast.98), calls=%async_computation.16 | async-start | bytes 8388608
  537.8 181.5 %collective-permute-start.1 = (f32[1024,2048]{1,0:T(8,128)}, f32[1024,2048]{1,0:T(8,128)}, u32[]{:S(2)}, u32[]{:S(2)}) collective-permute-start(f32[1024,2048]{1,0:T(8,128)} %add.249), channel_id=1, source_target_pairs={{0,2},{1,3},{2,0},{3,1},{4,6},{5,7},{6,4},{7,5},{8,10},{9,11},{10,... | collective-permute-start | bytes 25165832 | tf_op jit(solution)/shard_map/ppermute | solution.py:165
  539.1 180.2 %slice-start.1 = ((s8[8388608]{0:T(1024)(128)(4,1)}), s8[4194304]{0:T(1024)(128)(4,1)S(1)}, s32[]{:S(2)}) async-start(s8[8388608]{0:T(1024)(128)(4,1)} %bitcast.98), calls=%async_computation.17 | async-start | bytes 8388608
  539.1 180.2 %copy-start.3 = (f32[1024,2048]{1,0:T(8,128)S(1)}, f32[1024,2048]{1,0:T(8,128)}, u32[]{:S(2)}) copy-start(f32[1024,2048]{1,0:T(8,128)} %add.249) | copy-start | bytes 25165828
  553.9 171.1 %copy-start.19 = (bf16[1024,2048]{1,0:T(8,128)(2,1)S(1)}, bf16[1024,2048]{1,0:T(8,128)(2,1)}, u32[]{:S(2)}) copy-start(bf16[1024,2048]{1,0:T(8,128)(2,1)} %param.35) | copy-start | bytes 12582916
  740.7 22.9 %copy-start.44 = (bf16[512,512]{0,1:T(8,128)(2,1)}, bf16[512,512]{0,1:T(8,128)(2,1)S(1)}, u32[]{:S(2)}) copy-start(bf16[512,512]{0,1:T(8,128)(2,1)S(1)} %get-tuple-element.98) | copy-start | bytes 1572868
  798.1 364.4 %reduce-scatter.12.cloned.1.call-start = ((), (), s32[]{:S(2)}) async-start(), calls=%async_computation.10 | async-start | bytes 4718592 | tf_op jit(solution)/shard_map/reduce_scatter | solution.py:243
  806.0 405.9 %reduce-scatter.14.cloned.1.call-start = ((), (), s32[]{:S(2)}) async-start(), calls=%async_computation.11 | async-start | bytes 4718592 | tf_op jit(solution)/shard_map/reduce_scatter | solution.py:244
  813.9 449.2 %reduce-scatter.10.cloned.1.call-start = ((), (), s32[]{:S(2)}) async-start(), calls=%async_computation.9 | async-start | bytes 4718592 | tf_op jit(solution)/shard_map/reduce_scatter | solution.py:242
  821.0 493.2 %reduce-scatter.8.cloned.1.call-start = ((), (), s32[]{:S(2)}) async-start(), calls=%async_computation.8 | async-start | bytes 4718592 | tf_op jit(solution)/shard_map/reduce_scatter | solution.py:241
  828.3 655.4 %reduce-scatter.16.cloned.1.call-start = ((), (), s32[]{:S(2)}) async-start(), calls=%async_computation.12 | async-start | bytes 18874368 | tf_op jit(solution)/shard_map/reduce_scatter | solution.py:174
  844.3 809.1 %reduce-scatter.18.cloned.1.call-start = ((), (), s32[]{:S(2)}) async-start(), calls=%async_computation.13 | async-start | bytes 18874368 | tf_op jit(solution)/shard_map/reduce_scatter | solution.py:175
  859.8 963.1 %reduce-scatter.20.cloned.1.call-start = ((), (), s32[]{:S(2)}) async-start(), calls=%async_computation.14 | async-start | bytes 18874368 | tf_op jit(solution)/shard_map/reduce_scatter | solution.py:176
  875.8 236.4 %copy-start.49 = (f32[2048]{0:T(1024)S(1)}, f32[2048]{0:T(1024)}, u32[]{:S(2)}) copy-start(f32[2048]{0:T(1024)} %get-tuple-element.71) | copy-start | bytes 24580
  1143.1 679.9 %copy-start.1 = (bf16[512,2048]{1,0:T(8,128)(2,1)S(1)}, bf16[512,2048]{1,0:T(8,128)(2,1)}, u32[]{:S(2)}) copy-start(bf16[512,2048]{1,0:T(8,128)(2,1)} %param.30) | copy-start | bytes 6291460
  (54 other events, 363.3 us)
Sparse Core Ops, SparseCore 0:
  82.3 174.7 all-reduce.13
  798.2 308.0 all-reduce.15
  1109.2 51.4 reduce-scatter.11
  1163.4 48.4 reduce-scatter.13
  1214.6 48.3 reduce-scatter.9
  1265.8 48.3 reduce-scatter.7
  1317.1 166.6 reduce-scatter.15
  1486.7 166.6 reduce-scatter.17
  1656.3 166.6 reduce-scatter.19
